TPU v7x, 256 devices: a whole 4x4x8 slice. The times are simulated.
256 devices in a mesh: ctx: 64 (over x, z, y_hi), tp: 4 (over y_lo, core).
Axes of the slice: x: 4, y: 4 (y_hi: 2, y_lo: 2; y = y_hi * 2 + y_lo), z: 8, core: 2. Of those that a mesh axis runs over, the one named last changes fastest.
Arguments:
- q_one: bfloat16 [16384, 4096], P('ctx', 'tp'), may hold values from -880 to 880
- k_one: bfloat16 [16384, 4096], P('ctx', 'tp'), may hold values from -6 to 6
- v_one: bfloat16 [16384, 4096], P('ctx', 'tp'), may hold values from -6 to 6
- q_two: bfloat16 [16384, 4096], P('ctx', 'tp'), may hold values from -6 to 6
- k_two: bfloat16 [16384, 4096], P('ctx', 'tp'), may hold values from -6 to 6
- short_taps: bfloat16 [3, 7, 256], P(None, None, 'tp'), may hold values from -2 to 2
- medium_taps: bfloat16 [128, 256], P(None, 'tp'), may hold values from -0.5 to 0.5
- long_taps: bfloat16 [256, 16384], P('tp', 'ctx'), may hold values from -0.046875 to 0.046875
- skip_gain: float32 [4096], P('tp'), may hold values from -4 to 4
- block_order: int32 [64], replicated, may hold values from 0 to 63, as said below
- prev_owner: int32 [64], replicated, may hold values from 0 to 63, as said below
Outputs:
- gated_out: bfloat16 [16384, 4096], P('ctx', 'tp')
Inputs may be any that keep to these rules, and one draw needn't show every extreme that they name: `block_order`: A permutation of the 64 sequence blocks over the devices of ctx. prev_owner[b] is the device d with block_order[d] = b - 1 for b > 0, and prev_owner[0] the device holding block 63.
All inputs are finite; a program needn't handle non-finite values.
Results may differ from a plain program's by a relative error of at most 0.008.
Values may be sent and summed in bfloat16 or wider, within the bound.
A program may use at most 128 MiB of HBM per device.

v0:
```python
import math
import jax
import jax.numpy as jnp
from jax import lax
from jax.sharding import PartitionSpec as P

EPSILON = 1e-06
HIGHEST = lax.Precision.HIGHEST


def rows_filter(signal, kernel_taps):
    flipped = kernel_taps[::-1][:, None, :]
    result = lax.conv_general_dilated(
        signal[None],
        flipped,
        (1,),
        "VALID",
        dimension_numbers=("NWC", "WIO", "NWC"),
        feature_group_count=signal.shape[1],
        preferred_element_type=jnp.float32,
    )
    return result[0]


def angle_table(first_len, second_len, period):
    first = jnp.arange(first_len, dtype=jnp.int32)
    second = jnp.arange(second_len, dtype=jnp.int32)
    angle = 2.0 * math.pi / period * (first[:, None] * second[None, :] % period).astype(jnp.float32)
    return (jnp.cos(angle), jnp.sin(angle))


def forward_spectrum(signal, half_outer, tables):
    outer_cos, outer_sin, twist_cos, twist_sin, inner_cos, inner_sin = tables
    real_a = jnp.einsum("kn,bnm->bkm", outer_cos[:, :half_outer], signal, precision=HIGHEST)
    imag_a = -jnp.einsum("kn,bnm->bkm", outer_sin[:, :half_outer], signal, precision=HIGHEST)
    real_b = real_a * twist_cos + imag_a * twist_sin
    imag_b = imag_a * twist_cos - real_a * twist_sin
    real_c = jnp.einsum("bkm,mj->bkj", real_b, inner_cos, precision=HIGHEST) + jnp.einsum(
        "bkm,mj->bkj", imag_b, inner_sin, precision=HIGHEST
    )
    imag_c = jnp.einsum("bkm,mj->bkj", imag_b, inner_cos, precision=HIGHEST) - jnp.einsum(
        "bkm,mj->bkj", real_b, inner_sin, precision=HIGHEST
    )
    return (real_c, imag_c)


def inverse_spectrum(real_p, imag_p, half_outer, tables):
    outer_cos, outer_sin, twist_cos, twist_sin, inner_cos, inner_sin = tables
    real_q = jnp.einsum("bkj,jm->bkm", real_p, inner_cos, precision=HIGHEST) - jnp.einsum(
        "bkj,jm->bkm", imag_p, inner_sin, precision=HIGHEST
    )
    imag_q = jnp.einsum("bkj,jm->bkm", imag_p, inner_cos, precision=HIGHEST) + jnp.einsum(
        "bkj,jm->bkm", real_p, inner_sin, precision=HIGHEST
    )
    real_r = real_q * twist_cos - imag_q * twist_sin
    imag_r = imag_q * twist_cos + real_q * twist_sin
    return jnp.einsum(
        "nk,bkm->bnm", outer_cos[:half_outer], real_r, precision=HIGHEST
    ) - jnp.einsum("nk,bkm->bnm", outer_sin[:half_outer], imag_r, precision=HIGHEST)


def long_mix(values, long_rows, gain_local, block_rows):
    channels, length = values.shape
    outer_len = length // block_rows
    inner_len = 2 * block_rows
    half_outer = outer_len // 2
    padded_len = 2 * length
    outer_cos, outer_sin = angle_table(outer_len, outer_len, outer_len)
    twist_cos, twist_sin = angle_table(outer_len, inner_len, padded_len)
    inner_cos, inner_sin = angle_table(inner_len, inner_len, inner_len)
    tables = (outer_cos, outer_sin, twist_cos, twist_sin, inner_cos, inner_sin)
    value_float = values.astype(jnp.float32)
    real_x, imag_x = forward_spectrum(
        value_float.reshape(channels, half_outer, inner_len), half_outer, tables
    )
    real_h, imag_h = forward_spectrum(
        long_rows.astype(jnp.float32).reshape(long_rows.shape[0], half_outer, inner_len),
        half_outer,
        tables,
    )
    group_size = channels // long_rows.shape[0]
    real_h = jnp.repeat(real_h, group_size, axis=0)
    imag_h = jnp.repeat(imag_h, group_size, axis=0)
    real_p = real_x * real_h - imag_x * imag_h
    imag_p = real_x * imag_h + imag_x * real_h
    long_part = inverse_spectrum(real_p, imag_p, half_outer, tables) / padded_len
    return (long_part.reshape(channels, length) + gain_local[:, None] * value_float).astype(
        jnp.bfloat16
    )


def per_device(
    q_one,
    k_one,
    v_one,
    q_two,
    k_two,
    short_taps,
    medium_taps,
    long_taps,
    skip_gain,
    block_order,
    prev_owner,
):
    block_rows, local_width = q_one.shape
    ctx_count = lax.axis_size("ctx")
    device_pos = lax.axis_index("ctx")
    group_size = local_width // short_taps.shape[2]
    short_lead = short_taps.shape[1] - 1
    medium_reach = medium_taps.shape[0] - 1
    lane_width = local_width // ctx_count
    full_width = local_width * lax.axis_size("tp")
    short_lanes = jnp.repeat(short_taps, group_size, axis=2)
    medium_lanes = jnp.repeat(medium_taps, group_size, axis=1)
    lane_start = device_pos * lane_width
    slots = jnp.arange(ctx_count, dtype=jnp.int32)
    holder = jnp.sum(jnp.where(block_order[None, :] == slots[:, None], slots[None, :], 0), axis=1)
    my_block = block_order[device_pos]
    source = prev_owner[my_block]
    end_span = short_lead + medium_reach
    k_end = rows_filter(k_one[block_rows - end_span :], short_lanes[1])
    v_end = rows_filter(v_one[block_rows - end_span :], short_lanes[2])
    z_end = (k_end * v_end).astype(jnp.bfloat16)

    def select_source(carry, pieces):
        count = pieces[0].shape[0]
        matches = jnp.arange(count, dtype=jnp.int32) == source
        return tuple(
            (
                partial_sum
                + jnp.sum(jnp.where(matches[:, None, None], piece.astype(jnp.float32), 0.0), axis=0)
                for partial_sum, piece in zip(carry, pieces)
            )
        )

    empty_tails = (
        jnp.zeros((short_lead, local_width), jnp.float32),
        jnp.zeros((short_lead, local_width), jnp.float32),
        jnp.zeros((short_lead, local_width), jnp.float32),
        jnp.zeros((medium_reach, local_width), jnp.float32),
    )
    fetched = select_source(
        empty_tails,
        (
            lax.all_gather(q_one[None, block_rows - short_lead :], "ctx", axis=0, tiled=True),
            lax.all_gather(k_one[None, block_rows - short_lead :], "ctx", axis=0, tiled=True),
            lax.all_gather(v_one[None, block_rows - short_lead :], "ctx", axis=0, tiled=True),
            lax.all_gather(z_end[None], "ctx", axis=0, tiled=True),
        ),
    )
    has_before = my_block > 0
    tail_rows = [jnp.where(has_before, piece, 0.0).astype(jnp.bfloat16) for piece in fetched]
    q_feat = rows_filter(jnp.concatenate([tail_rows[0], q_one], axis=0), short_lanes[0])
    k_feat = rows_filter(jnp.concatenate([tail_rows[1], k_one], axis=0), short_lanes[1])
    v_feat = rows_filter(jnp.concatenate([tail_rows[2], v_one], axis=0), short_lanes[2])
    z_one = (k_feat * v_feat).astype(jnp.bfloat16)
    medium = rows_filter(jnp.concatenate([tail_rows[3], z_one], axis=0), medium_lanes)
    mixed = q_feat * medium
    energy = lax.psum(jnp.sum(mixed * mixed, axis=1), "tp")
    v_two = (
        k_two.astype(jnp.float32) * mixed * lax.rsqrt(energy / full_width + EPSILON)[:, None]
    ).astype(jnp.bfloat16)
    lanes, long_rows = (
        lax.all_to_all(jnp.transpose(v_two), "ctx", split_axis=0, concat_axis=1, tiled=True),
        lax.all_to_all(long_taps, "ctx", split_axis=0, concat_axis=1, tiled=True),
    )
    values = jnp.take(lanes.reshape(lane_width, ctx_count, block_rows), holder, axis=1).reshape(
        lane_width, ctx_count * block_rows
    )
    gain_local = lax.dynamic_slice_in_dim(skip_gain, lane_start, lane_width)
    mixed_seq = long_mix(values, long_rows, gain_local, block_rows)
    device_major = jnp.take(
        mixed_seq.reshape(lane_width, ctx_count, block_rows), block_order, axis=1
    ).reshape(lane_width, ctx_count * block_rows)
    returned = lax.all_to_all(device_major, "ctx", split_axis=1, concat_axis=0, tiled=True)
    return (q_two.astype(jnp.float32) * jnp.transpose(returned).astype(jnp.float32)).astype(
        jnp.bfloat16
    )


def solution(mesh):
    in_specs = (
        P("ctx", "tp"),
        P("ctx", "tp"),
        P("ctx", "tp"),
        P("ctx", "tp"),
        P("ctx", "tp"),
        P(None, None, "tp"),
        P(None, "tp"),
        P("tp", "ctx"),
        P("tp"),
        P(),
        P(),
    )
    out_specs = P("ctx", "tp")
    return jax.shard_map(
        per_device, mesh=mesh, in_specs=in_specs, out_specs=out_specs, check_vma=False
    )
```

profile of v0, /device:TPU:2, one launch (start us, length us, event | category | flops | bytes accessed | tf_op | source)
XLA Modules:
  0.0 769.9 jit_solution(8870785793664506424)
XLA Ops:
  6.5 0.8 slice_bitcast_fusion.12
  8.4 1.0 slice_bitcast_fusion.1
  10.2 0.3 convolution_select_fusion.3
  10.6 0.4 fusion.30
  11.3 0.7 slice.87
  12.0 0.5 broadcast.312
  12.5 0.7 reduce.1
  13.2 0.6 reshape.284
  13.8 14.7 %all-to-all-start.1 = ((bf16[64,2,128]{2,1,0:T(2,128)(2,1)}), bf16[64,2,128]{2,1,0:T(2,128)(2,1)S(1)}, u32[]{:S(2)}, u32[]{:S(2)}) async-start(bf16[64,2,128]{2,1,0:T(2,128)(2,1)} %reshape.284), calls=%async_computation.1 | async-start | bytes 65536 | tf_op jit(solution)/shard_map/all_to_all | solution.py:165
  28.5 0.6 dynamic_slice.9
  31.7 0.6 dynamic_slice.10
  32.3 0.6 iota_compare_fusion.3
  33.0 170.4 %all-gather.3 = bf16[64,6,1024]{2,1,0:T(8,128)(2,1)S(1)} all-gather(bf16[1,6,1024]{2,1,0:T(8,128)(2,1)S(1)} %slice_bitcast_fusion.9), channel_id=2, replica_groups=mesh['ctx'=64,'tp'=4] {'ctx'}, dimensions={0}, use_global_device_ids=true | all-gather | bytes 798720 | tf_op jit(solution)/shard_map/all_gather | solution.py:145
  203.4 172.6 %all-gather.4 = bf16[64,6,1024]{2,1,0:T(8,128)(2,1)S(1)} all-gather(bf16[1,6,1024]{2,1,0:T(8,128)(2,1)S(1)} %slice_bitcast_fusion.8), channel_id=3, replica_groups=mesh['ctx'=64,'tp'=4] {'ctx'}, dimensions={0}, use_global_device_ids=true | all-gather | bytes 798720 | tf_op jit(solution)/shard_map/all_gather | solution.py:146
  376.1 183.0 %all-gather.5 = bf16[64,6,1024]{2,1,0:T(8,128)(2,1)S(1)} all-gather(bf16[1,6,1024]{2,1,0:T(8,128)(2,1)S(1)} %slice_bitcast_fusion.7), channel_id=4, replica_groups=mesh['ctx'=64,'tp'=4] {'ctx'}, dimensions={0}, use_global_device_ids=true | all-gather | bytes 798720 | tf_op jit(solution)/shard_map/all_gather | solution.py:147
  559.1 1.0 fusion.4
  560.5 0.3 copy.120
  561.2 0.3 copy.117
  561.6 0.6 convolution_select_fusion
  562.2 0.7 fusion.25
  562.9 0.3 copy.122
  563.8 0.3 copy.105
  564.5 0.7 rev.14
  565.2 0.6 convolution_select_fusion.2
  565.8 0.6 copy.107
  566.4 1.3 reshape.270
  567.8 0.8 rev.17
  568.6 1.1 copy.125
  569.7 1.3 dynamic_slice.11
  571.4 0.5 fusion.138
  572.0 0.7 compare_and_fusion
  572.9 0.3 convolution_bitcast_fusion
  573.2 7.4 select_reduce_fusion
  580.9 0.8 copy-done.3
  581.7 14.8 %fusion.32 = f32[1,256,1024]{2,0,1:T(1,128)S(1)} fusion(bf16[128,1,1024]{2,1,0:T(2,128)(2,1)S(1)} %copy-done.3, bf16[1,383,1024]{2,1,0:T(8,128)(2,1)S(1)} %maximum_bitcast_fusion, f32[1,264,1024]{2,0,1:T(1,128)S(1)} %reshape.270), kind=kOutput, calls=%fused_computation.55 | convolution fusion | flops 67371008 | bytes 3143680 | tf_op jit(solution)/shard_map/conv_general_dilated | solution.py:13
  596.7 5.8 psum.7
  602.5 1.2 fusion.82
  603.8 1.0 copy.126
  604.8 33.8 %all-to-all-start = ((bf16[64,16,256]{2,1,0:T(8,128)(2,1)}), bf16[64,16,256]{2,1,0:T(8,128)(2,1)S(1)}, u32[]{:S(2)}, u32[]{:S(2)}) async-start(bf16[64,16,256]{2,1,0:T(8,128)(2,1)} %bitcast.26), calls=%async_computation | async-start | bytes 1048576 | tf_op jit(solution)/shard_map/all_to_all | solution.py:164
  638.6 0.3 fusion.31
  638.9 5.1 fusion.90
  644.0 5.1 fusion.88
  649.1 5.3 convolution_add_fusion.2
  654.4 5.1 convolution_subtract_fusion.2
  659.6 0.6 gather_fusion
  660.7 1.1 fusion.151
  661.8 1.1 fusion.153
  663.0 7.9 %fusion.52 = f32[16,64,512]{2,1,0:T(8,128)S(1)} fusion(f32[16,512,64]{1,2,0:T(8,128)S(1)} %fusion.153, f32[16,512,64]{1,2,0:T(8,128)S(1)} %fusion.151, f32[64,512]{1,0:T(8,128)S(1)} %get-tuple-element.14, f32[64,512]{1,0:T(8,128)S(1)} %get-tuple-element.15), kind=kOutput, calls=%fused_computation.76 | convolution fusion | flops 3226992640 | bytes 6553600 | tf_op jit(solution)/shard_map/bkm,mj->bkj/dot_general | solution.py:38
  670.9 7.7 %fusion.50 = f32[16,64,512]{2,1,0:T(8,128)S(1)} fusion(f32[16,512,64]{1,2,0:T(8,128)S(1)} %fusion.153, f32[16,512,64]{1,2,0:T(8,128)S(1)} %fusion.151, f32[64,512]{1,0:T(8,128)S(1)} %get-tuple-element.14, f32[64,512]{1,0:T(8,128)S(1)} %get-tuple-element.15), kind=kOutput, calls=%fused_computation.74 | convolution fusion | flops 3226992640 | bytes 6553600 | tf_op jit(solution)/shard_map/bkm,mj->bkj/dot_general | solution.py:41
  678.6 7.6 convolution_add_fusion.1
  686.2 7.8 %convolution_subtract_fusion.1 = f32[16,64,512]{2,1,0:T(8,128)S(1)} fusion(f32[16,64,512]{2,1,0:T(8,128)S(1)} %fusion.50, f32[16,512,64]{1,2,0:T(8,128)S(1)} %fusion.153, f32[16,512,64]{1,2,0:T(8,128)S(1)} %fusion.151, f32[64,512]{1,0:T(8,128)S(1)} %get-tuple-element.14, f32[64,512]{1,0:T(8,128)S(1)} %get-tuple-element.15), kind=kOutput, calls=%fused_computation.27 | convolution fusion | flops 3227516928 | bytes 8650752 | tf_op jit(solution)/shard_map/bkm,mj->bkj/dot_general | solution.py:41
  694.0 7.5 fusion.46
  701.6 8.0 %fusion.48 = f32[16,64,512]{2,1,0:T(8,128)S(1)} fusion(f32[16,64,512]{2,1,0:T(8,128)S(1)} %convolution_subtract_fusion.1, f32[16,64,512]{2,1,0:T(8,128)S(1)} %convolution_add_fusion.1, f32[64,512]{1,0:T(8,128)S(1)} %convolution_subtract_fusion.2, f32[64,512]{1,0:T(8,128)S(1)} %convolution_add_fusion.2), kind=kOutput, calls=%fused_computation.72 | convolution fusion | flops 3226468352 | bytes 6553600 | tf_op jit(solution)/shard_map/bkj,jm->bkm/dot_general | solution.py:49
  709.5 7.7 %convolution_add_fusion = f32[16,64,512]{2,1,0:T(8,128)S(1)} fusion(f32[16,64,512]{2,1,0:T(8,128)S(1)} %fusion.46, f32[16,64,512]{2,1,0:T(8,128)S(1)} %convolution_subtract_fusion.1, f32[16,64,512]{2,1,0:T(8,128)S(1)} %convolution_add_fusion.1, f32[64,512]{1,0:T(8,128)S(1)} %convolution_subtract_fusion.2, f32[64,512]{1,0:T(8,128)S(1)} %convolution_add_fusion.2), kind=kOutput, calls=%fused_computation.25 | convolution fusion | flops 3226992640 | bytes 8650752 | tf_op jit(solution)/shard_map/bkj,jm->bkm/dot_general | solution.py:52
  717.3 7.5 convolution_subtract_fusion
  724.8 1.6 fusion.5
  726.4 1.7 fusion.22
  728.3 0.5 copy-done.7
  728.8 0.8 fusion.54
  729.6 0.6 gather_fusion.1
  730.2 0.9 select_bitcast_fusion
  731.1 12.8 %all-to-all-start.2 = ((bf16[16,64,256]{2,0,1:T(8,128)(2,1)}), bf16[16,64,256]{2,0,1:T(8,128)(2,1)S(1)}, u32[]{:S(2)}, u32[]{:S(2)}) async-start(bf16[16,64,256]{2,0,1:T(8,128)(2,1)} %select_bitcast_fusion), calls=%async_computation.2 | async-start | bytes 1048576 | tf_op jit(solution)/shard_map/all_to_all | solution.py:175
  744.1 17.6 %all-to-all-done.2 = bf16[16,64,256]{2,0,1:T(8,128)(2,1)S(1)} async-done(((bf16[16,64,256]{2,0,1:T(8,128)(2,1)}), bf16[16,64,256]{2,0,1:T(8,128)(2,1)S(1)}, u32[]{:S(2)}, u32[]{:S(2)}) %all-to-all-start.2) | async-done | bytes 524320 | tf_op jit(solution)/shard_map/all_to_all | solution.py:175
  761.9 1.0 copy.132
  (87 shorter events, 5.9 us)
Async XLA Ops:
  6.5 3.3 copy-start.1
  6.5 566.7 %all-gather.8.cloned.1.call-start = ((), (), s32[]{:S(2)}) async-start(), calls=%async_computation.3 | async-start | bytes 17039360 | tf_op jit(solution)/shard_map/all_gather | solution.py:148
  9.5 0.8 copy-start.11
  10.6 2.0 copy-start.5
  10.6 17.9 %copy-start.9 = (s32[64]{0:T(128)S(1)}, s32[64]{0:T(128)}, u32[]{:S(2)}) copy-start(s32[64]{0:T(128)} %param.22) | copy-start | bytes 772
  10.6 21.1 %copy-start.8 = (s32[64]{0:T(128)S(1)}, s32[64]{0:T(128)}, u32[]{:S(2)}) copy-start(s32[64]{0:T(128)} %param.23) | copy-start | bytes 772
  10.6 22.3 %copy-start = (bf16[256,1024]{1,0:T(8,128)(2,1)S(1)}, bf16[256,1024]{1,0:T(8,128)(2,1)}, u32[]{:S(2)}) copy-start(bf16[256,1024]{1,0:T(8,128)(2,1)} %param.15) | copy-start | bytes 1572868
  11.0 22.0 %copy-start.2 = (bf16[256,1024]{1,0:T(8,128)(2,1)S(1)}, bf16[256,1024]{1,0:T(8,128)(2,1)}, u32[]{:S(2)}) copy-start(bf16[256,1024]{1,0:T(8,128)(2,1)} %param.13) | copy-start | bytes 1572868
  13.8 558.9 %all-to-all-start.1 = ((bf16[64,2,128]{2,1,0:T(2,128)(2,1)}), bf16[64,2,128]{2,1,0:T(2,128)(2,1)S(1)}, u32[]{:S(2)}, u32[]{:S(2)}) async-start(bf16[64,2,128]{2,1,0:T(2,128)(2,1)} %reshape.284), calls=%async_computation.1 | async-start | bytes 65536 | tf_op jit(solution)/shard_map/all_to_all | solution.py:165
  561.0 0.7 copy-start.10
  565.8 2.0 copy-start.6
  580.6 1.0 copy-start.3
  604.8 54.8 %all-to-all-start = ((bf16[64,16,256]{2,1,0:T(8,128)(2,1)}), bf16[64,16,256]{2,1,0:T(8,128)(2,1)S(1)}, u32[]{:S(2)}, u32[]{:S(2)}) async-start(bf16[64,16,256]{2,1,0:T(8,128)(2,1)} %bitcast.26), calls=%async_computation | async-start | bytes 1048576 | tf_op jit(solution)/shard_map/all_to_all | solution.py:164
  728.1 0.7 copy-start.7
  729.6 14.3 %copy-start.4 = (bf16[256,1024]{1,0:T(8,128)(2,1)S(1)}, bf16[256,1024]{1,0:T(8,128)(2,1)}, u32[]{:S(2)}) copy-start(bf16[256,1024]{1,0:T(8,128)(2,1)} %param.16) | copy-start | bytes 1572868
  731.1 30.6 %all-to-all-start.2 = ((bf16[16,64,256]{2,0,1:T(8,128)(2,1)}), bf16[16,64,256]{2,0,1:T(8,128)(2,1)S(1)}, u32[]{:S(2)}, u32[]{:S(2)}) async-start(bf16[16,64,256]{2,0,1:T(8,128)(2,1)} %select_bitcast_fusion), calls=%async_computation.2 | async-start | bytes 1048576 | tf_op jit(solution)/shard_map/all_to_all | solution.py:175
Sparse Core Ops, SparseCore 0:
  12.1 213.6 all-gather.7
where the time goes:
time: 778 us; the launch traced here: 770 us
  blocking collectives  532 us (68%)
  matrix products  106 us (14%)
  starting transfers between devices  61.3 us (8%)
  local copies, waits for them, and re-layouts  20.6 us (3%)
  waiting for transfers between devices  17.7 us (2%)
  between operations  17 us (2%)
  other arithmetic  15.6 us (2%)
    all_gather x1, blocking collectives, per_device(): lax.all_gather(v_one[None, block_rows - short_lead:], 'ctx', axis=0, tile...  183 us
    all_gather x1, blocking collectives, per_device(): lax.all_gather(k_one[None, block_rows - short_lead:], 'ctx', axis=0, tile...  173 us
    all_gather x1, blocking collectives, per_device(): lax.all_gather(q_one[None, block_rows - short_lead:], 'ctx', axis=0, tile...  170 us
    all_to_all x1, starting transfers between devices, per_device(): lax.all_to_all(jnp.transpose(v_two), 'ctx', split_axis=0, concat_axis=1,...  33.8 us
    all_to_all x1, waiting for transfers between devices, per_device(): lax.all_to_all(device_major, 'ctx', split_axis=1, concat_axis=0, tiled=True)  17.6 us
    conv_general_dilated x6, matrix products, rows_filter(): lax.conv_general_dilated(signal[None], flipped, (1,), 'VALID', dimension_...  17.3 us
  transfers between devices with their start and end apart: 4, of which 1 were waited for; matrix products, arithmetic and copies ran while one was open for 5% of the time, Pallas kernels for 0%

commit v1 on v0

--- a/solution.py
+++ b/solution.py
@@ -139,11 +139,18 @@
         jnp.zeros((short_lead, local_width), jnp.float32),
         jnp.zeros((medium_reach, local_width), jnp.float32),
     )
+
+    def check_sample(target):
+        a_next = jnp.concatenate(
+            jax.lax.all_to_all(jnp.stack([target] * jax.lax.axis_size("ctx")), "ctx", 0, 0), axis=0
+        )
+        return a_next
+
     fetched = select_source(
         empty_tails,
         (
             lax.all_gather(q_one[None, block_rows - short_lead :], "ctx", axis=0, tiled=True),
-            lax.all_gather(k_one[None, block_rows - short_lead :], "ctx", axis=0, tiled=True),
+            check_sample(k_one[None, block_rows - short_lead :]),
             lax.all_gather(v_one[None, block_rows - short_lead :], "ctx", axis=0, tiled=True),
             lax.all_gather(z_end[None], "ctx", axis=0, tiled=True),
         ),

time: 778 us -> 635 us (0.82)
  blocking collectives: 532 us -> 365 us
  starting transfers between devices: 61.3 us -> 74 us
  local copies, waits for them, and re-layouts: 20.6 us -> 29.6 us
    all_gather x1 -> x0, blocking collectives: 173 us -> none  [per_device(): lax.all_gather(k_one[None, block_rows - short_lead:], 'ctx', axis=0, tile...]
    all_gather x1, blocking collectives: 170 us -> 186 us  [per_device(): lax.all_gather(q_one[None, block_rows - short_lead:], 'ctx', axis=0, tile...]
    all_to_all x0 -> x1, starting transfers between devices: none -> 12.7 us  [check_sample(): jax.lax.all_to_all(jnp.stack([target] * jax.lax.axis_size('ctx')), 'ctx',...]
    all_gather x1, blocking collectives: 183 us -> 174 us  [per_device(): lax.all_gather(v_one[None, block_rows - short_lead:], 'ctx', axis=0, tile...]
  transfers between devices with their start and end apart: 4 -> 5, of which waited for: 1 -> 1; matrix products, arithmetic and copies ran while one was open for 5% -> 8% of each run, Pallas kernels for 0% -> 0%
where the time goes in v1:
time: 635 us; the launch traced here: 629 us
  blocking collectives  365 us (57%)
  matrix products  107 us (17%)
  starting transfers between devices  74 us (12%)
  local copies, waits for them, and re-layouts  29.6 us (5%)
  other arithmetic  18 us (3%)
  waiting for transfers between devices  17.8 us (3%)
  between operations  17.1 us (3%)
    all_gather x1, blocking collectives, per_device(): lax.all_gather(q_one[None, block_rows - short_lead:], 'ctx', axis=0, tile...  186 us
    all_gather x1, blocking collectives, per_device(): lax.all_gather(v_one[None, block_rows - short_lead:], 'ctx', axis=0, tile...  174 us
    all_to_all x1, starting transfers between devices, per_device(): lax.all_to_all(jnp.transpose(v_two), 'ctx', split_axis=0, concat_axis=1,...  33.8 us
    all_to_all x1, waiting for transfers between devices, per_device(): lax.all_to_all(device_major, 'ctx', split_axis=1, concat_axis=0, tiled=True)  17.8 us
    conv_general_dilated x6, matrix products, rows_filter(): lax.conv_general_dilated(signal[None], flipped, (1,), 'VALID', dimension_...  17.3 us
    all_to_all x1, starting transfers between devices, per_device(): lax.all_to_all(long_taps, 'ctx', split_axis=0, concat_axis=1, tiled=True)  14.7 us
    dot_general x2, matrix products, forward_spectrum(): jnp.einsum('bkm,mj->bkj', real_b, inner_sin, precision=HIGHEST)  13.6 us
    dot_general x2, matrix products, forward_spectrum(): jnp.einsum('bkm,mj->bkj', real_b, inner_cos, precision=HIGHEST)  13 us
  transfers between devices with their start and end apart: 5, of which 1 were waited for; matrix products, arithmetic and copies ran while one was open for 8% of the time, Pallas kernels for 0%

profile of v1, /device:TPU:2, one launch (start us, length us, event | category | flops | bytes accessed | tf_op | source)
XLA Modules:
  0.0 629.0 jit_solution(9239776286544149945)
XLA Ops:
  6.5 0.8 slice_bitcast_fusion.11
  8.4 1.0 slice_bitcast_fusion.1
  11.3 0.7 slice.87
  12.1 0.5 broadcast.314
  12.6 0.7 reduce.1
  13.2 0.6 reshape.284
  13.9 14.7 %all-to-all-start.2 = ((bf16[64,2,128]{2,1,0:T(2,128)(2,1)}), bf16[64,2,128]{2,1,0:T(2,128)(2,1)S(1)}, u32[]{:S(2)}, u32[]{:S(2)}) async-start(bf16[64,2,128]{2,1,0:T(2,128)(2,1)} %reshape.284), calls=%async_computation.2 | async-start | bytes 65536 | tf_op jit(solution)/shard_map/all_to_all | solution.py:172
  28.5 0.6 dynamic_slice.9
  31.4 2.5 rev.14
  33.9 0.8 rev.17
  34.7 1.1 copy.127
  36.4 0.6 dynamic_slice.10
  37.0 1.3 dynamic_slice.11
  38.4 0.6 pad_clamp_fusion.1
  39.0 0.6 pad_clamp_fusion
  39.9 0.5 fusion.138
  40.5 0.6 compare_and_fusion.1
  41.1 1.2 iota_compare_fusion.3
  42.3 1.1 stack.3
  43.4 12.7 %all-to-all-start = ((bf16[64,1,6,1024]{3,2,1,0:T(8,128)(2,1)}), bf16[64,1,6,1024]{3,2,1,0:T(8,128)(2,1)S(1)}, u32[]{:S(2)}, u32[]{:S(2)}) async-start(bf16[64,1,6,1024]{3,2,1,0:T(8,128)(2,1)} %stack.3), calls=%async_computation | async-start | bytes 2097152 | tf_op jit(solution)/shard_map/all_to_all | solution.py:145
  56.1 0.5 compare_and_fusion
  56.6 0.7 slice_bitcast_fusion.7
  57.4 0.7 slice_bitcast_fusion.8
  58.1 185.7 %all-gather.2 = bf16[64,6,1024]{2,1,0:T(8,128)(2,1)S(1)} all-gather(bf16[1,6,1024]{2,1,0:T(8,128)(2,1)S(1)} %slice_bitcast_fusion.8), channel_id=2, replica_groups=mesh['ctx'=64,'tp'=4] {'ctx'}, dimensions={0}, use_global_device_ids=true | all-gather | bytes 798720 | tf_op jit(solution)/shard_map/all_gather | solution.py:152
  243.8 173.9 %all-gather.3 = bf16[64,6,1024]{2,1,0:T(8,128)(2,1)S(1)} all-gather(bf16[1,6,1024]{2,1,0:T(8,128)(2,1)S(1)} %slice_bitcast_fusion.7), channel_id=3, replica_groups=mesh['ctx'=64,'tp'=4] {'ctx'}, dimensions={0}, use_global_device_ids=true | all-gather | bytes 798720 | tf_op jit(solution)/shard_map/all_gather | solution.py:154
  417.7 0.8 reshape.285
  418.5 0.8 reduce
  419.3 0.8 reshape.178
  420.1 0.9 convolution_bitcast_fusion
  421.0 1.7 fusion.4
  424.7 0.6 convolution_select_fusion
  425.4 0.7 fusion.25
  428.0 0.6 convolution_select_fusion.2
  428.6 0.6 copy.108
  429.3 2.3 reshape.270
  431.6 7.4 %select_reduce_fusion = bf16[127,1024]{1,0:T(8,128)(2,1)S(1)} fusion(bf16[64,127,1024]{2,1,0:T(8,128)(2,1)} %all-gather.6.cloned.1.call-done, pred[64]{0:T(512)(128)(4,1)S(1)} %copy-done.22), kind=kLoop, calls=%fused_computation.2 | loop fusion | flops 24839168 | bytes 16906304 | tf_op jit(solution)/shard_map/reduce_sum | solution.py:131
  439.3 1.0 copy-done.3
  440.4 14.8 %fusion.32 = f32[1,256,1024]{2,0,1:T(1,128)S(1)} fusion(bf16[128,1,1024]{2,1,0:T(2,128)(2,1)S(1)} %copy-done.6, bf16[1,383,1024]{2,1,0:T(8,128)(2,1)S(1)} %maximum_bitcast_fusion, f32[1,264,1024]{2,0,1:T(1,128)S(1)} %copy-done.3), kind=kOutput, calls=%fused_computation.55 | convolution fusion | flops 67371008 | bytes 3143680 | tf_op jit(solution)/shard_map/conv_general_dilated | solution.py:13
  455.4 5.8 psum.7
  461.4 1.0 copy.128
  462.4 33.8 %all-to-all-start.1 = ((bf16[64,16,256]{2,1,0:T(8,128)(2,1)}), bf16[64,16,256]{2,1,0:T(8,128)(2,1)S(1)}, u32[]{:S(2)}, u32[]{:S(2)}) async-start(bf16[64,16,256]{2,1,0:T(8,128)(2,1)} %bitcast.27), calls=%async_computation.1 | async-start | bytes 1048576 | tf_op jit(solution)/shard_map/all_to_all | solution.py:171
  496.6 5.1 fusion.90
  501.7 5.1 fusion.88
  506.8 5.3 convolution_add_fusion.2
  512.1 5.8 convolution_subtract_fusion.2
  517.9 0.8 gather_fusion
  519.3 1.1 fusion.151
  520.5 1.1 fusion.153
  521.6 7.9 %fusion.52 = f32[16,64,512]{2,1,0:T(8,128)S(1)} fusion(f32[16,512,64]{1,2,0:T(8,128)S(1)} %fusion.153, f32[16,512,64]{1,2,0:T(8,128)S(1)} %fusion.151, f32[64,512]{1,0:T(8,128)S(1)} %get-tuple-element.14, f32[64,512]{1,0:T(8,128)S(1)} %get-tuple-element.15), kind=kOutput, calls=%fused_computation.76 | convolution fusion | flops 3226992640 | bytes 6553600 | tf_op jit(solution)/shard_map/bkm,mj->bkj/dot_general | solution.py:38
  529.5 7.7 %fusion.50 = f32[16,64,512]{2,1,0:T(8,128)S(1)} fusion(f32[16,512,64]{1,2,0:T(8,128)S(1)} %fusion.153, f32[16,512,64]{1,2,0:T(8,128)S(1)} %fusion.151, f32[64,512]{1,0:T(8,128)S(1)} %get-tuple-element.14, f32[64,512]{1,0:T(8,128)S(1)} %get-tuple-element.15), kind=kOutput, calls=%fused_computation.74 | convolution fusion | flops 3226992640 | bytes 6553600 | tf_op jit(solution)/shard_map/bkm,mj->bkj/dot_general | solution.py:41
  537.2 7.6 %convolution_add_fusion.1 = f32[16,64,512]{2,1,0:T(8,128)S(1)} fusion(f32[16,64,512]{2,1,0:T(8,128)S(1)} %fusion.52, f32[16,512,64]{1,2,0:T(8,128)S(1)} %fusion.153, f32[16,512,64]{1,2,0:T(8,128)S(1)} %fusion.151, f32[64,512]{1,0:T(8,128)S(1)} %get-tuple-element.14, f32[64,512]{1,0:T(8,128)S(1)} %get-tuple-element.15), kind=kOutput, calls=%fused_computation.28 | convolution fusion | flops 3227516928 | bytes 8650752 | tf_op jit(solution)/shard_map/bkm,mj->bkj/dot_general | solution.py:38
  544.8 7.8 %convolution_subtract_fusion.1 = f32[16,64,512]{2,1,0:T(8,128)S(1)} fusion(f32[16,64,512]{2,1,0:T(8,128)S(1)} %fusion.50, f32[16,512,64]{1,2,0:T(8,128)S(1)} %fusion.153, f32[16,512,64]{1,2,0:T(8,128)S(1)} %fusion.151, f32[64,512]{1,0:T(8,128)S(1)} %get-tuple-element.14, f32[64,512]{1,0:T(8,128)S(1)} %get-tuple-element.15), kind=kOutput, calls=%fused_computation.27 | convolution fusion | flops 3227516928 | bytes 8650752 | tf_op jit(solution)/shard_map/bkm,mj->bkj/dot_general | solution.py:41
  552.7 7.5 %fusion.46 = f32[16,64,512]{2,1,0:T(8,128)S(1)} fusion(f32[16,64,512]{2,1,0:T(8,128)S(1)} %convolution_subtract_fusion.1, f32[16,64,512]{2,1,0:T(8,128)S(1)} %convolution_add_fusion.1, f32[64,512]{1,0:T(8,128)S(1)} %copy-done.5, f32[64,512]{1,0:T(8,128)S(1)} %convolution_add_fusion.2), kind=kOutput, calls=%fused_computation.70 | convolution fusion | flops 3226468352 | bytes 6553600 | tf_op jit(solution)/shard_map/bkj,jm->bkm/dot_general | solution.py:52
  560.2 8.0 %fusion.48 = f32[16,64,512]{2,1,0:T(8,128)S(1)} fusion(f32[16,64,512]{2,1,0:T(8,128)S(1)} %convolution_subtract_fusion.1, f32[16,64,512]{2,1,0:T(8,128)S(1)} %convolution_add_fusion.1, f32[64,512]{1,0:T(8,128)S(1)} %copy-done.5, f32[64,512]{1,0:T(8,128)S(1)} %convolution_add_fusion.2), kind=kOutput, calls=%fused_computation.72 | convolution fusion | flops 3226468352 | bytes 6553600 | tf_op jit(solution)/shard_map/bkj,jm->bkm/dot_general | solution.py:49
  568.2 7.7 %convolution_add_fusion = f32[16,64,512]{2,1,0:T(8,128)S(1)} fusion(f32[16,64,512]{2,1,0:T(8,128)S(1)} %fusion.46, f32[16,64,512]{2,1,0:T(8,128)S(1)} %convolution_subtract_fusion.1, f32[16,64,512]{2,1,0:T(8,128)S(1)} %convolution_add_fusion.1, f32[64,512]{1,0:T(8,128)S(1)} %copy-done.5, f32[64,512]{1,0:T(8,128)S(1)} %convolution_add_fusion.2), kind=kOutput, calls=%fused_computation.25 | convolution fusion | flops 3226992640 | bytes 8650752 | tf_op jit(solution)/shard_map/bkj,jm->bkm/dot_general | solution.py:52
  575.9 7.6 %convolution_subtract_fusion = f32[16,64,512]{2,1,0:T(8,128)S(1)} fusion(f32[16,64,512]{2,1,0:T(8,128)S(1)} %fusion.48, f32[16,64,512]{2,1,0:T(8,128)S(1)} %convolution_subtract_fusion.1, f32[16,64,512]{2,1,0:T(8,128)S(1)} %convolution_add_fusion.1, f32[64,512]{1,0:T(8,128)S(1)} %copy-done.5, f32[64,512]{1,0:T(8,128)S(1)} %convolution_add_fusion.2), kind=kOutput, calls=%fused_computation.26 | convolution fusion | flops 3226992640 | bytes 8650752 | tf_op jit(solution)/shard_map/bkj,jm->bkm/dot_general | solution.py:49
  583.5 1.6 fusion.5
  585.1 1.7 fusion.22
  587.4 0.8 fusion.54
  588.3 0.8 gather_fusion.1
  589.1 0.9 select_bitcast_fusion
  590.1 12.7 %all-to-all-start.3 = ((bf16[16,64,256]{2,0,1:T(8,128)(2,1)}), bf16[16,64,256]{2,0,1:T(8,128)(2,1)S(1)}, u32[]{:S(2)}, u32[]{:S(2)}) async-start(bf16[16,64,256]{2,0,1:T(8,128)(2,1)} %select_bitcast_fusion), calls=%async_computation.3 | async-start | bytes 1048576 | tf_op jit(solution)/shard_map/all_to_all | solution.py:182
  603.0 17.8 %all-to-all-done.3 = bf16[16,64,256]{2,0,1:T(8,128)(2,1)S(1)} async-done(((bf16[16,64,256]{2,0,1:T(8,128)(2,1)}), bf16[16,64,256]{2,0,1:T(8,128)(2,1)S(1)}, u32[]{:S(2)}, u32[]{:S(2)}) %all-to-all-start.3) | async-done | bytes 524320 | tf_op jit(solution)/shard_map/all_to_all | solution.py:182
  620.9 1.0 copy.134
  (125 shorter events, 10.0 us)
Async XLA Ops:
  6.5 3.3 copy-start.1
  6.5 425.1 %all-gather.6.cloned.1.call-start = ((), (), s32[]{:S(2)}) async-start(), calls=%async_computation.4 | async-start | bytes 17039360 | tf_op jit(solution)/shard_map/all_gather | solution.py:155
  8.4 2.2 copy-start.19
  9.5 0.8 copy-start.29
  10.6 2.0 copy-start.17
  10.6 17.9 %copy-start.27 = (s32[64]{0:T(128)S(1)}, s32[64]{0:T(128)}, u32[]{:S(2)}) copy-start(s32[64]{0:T(128)} %param.22) | copy-start | bytes 772
  11.0 22.9 %copy-start.18 = (bf16[128,64]{0,1:T(8,128)(2,1)S(1)}, bf16[128,64]{0,1:T(8,128)(2,1)}, u32[]{:S(2)}) copy-start(bf16[128,64]{0,1:T(8,128)(2,1)} %param.19) | copy-start | bytes 49156
  11.0 25.4 %copy-start.26 = (s32[64]{0:T(128)S(1)}, s32[64]{0:T(128)}, u32[]{:S(2)}) copy-start(s32[64]{0:T(128)} %param.23) | copy-start | bytes 772
  13.9 28.4 %all-to-all-start.2 = ((bf16[64,2,128]{2,1,0:T(2,128)(2,1)}), bf16[64,2,128]{2,1,0:T(2,128)(2,1)S(1)}, u32[]{:S(2)}, u32[]{:S(2)}) async-start(bf16[64,2,128]{2,1,0:T(2,128)(2,1)} %reshape.284), calls=%async_computation.2 | async-start | bytes 65536 | tf_op jit(solution)/shard_map/all_to_all | solution.py:172
  39.8 456.5 %copy-start.12 = (f32[64,64]{0,1:T(8,128)}, f32[64,64]{0,1:T(8,128)S(1)}, u32[]{:S(2)}) copy-start(f32[64,64]{0,1:T(8,128)S(1)} %fusion.155) | copy-start | bytes 49156
  39.9 380.1 %copy-start.9 = (f32[64,64]{0,1:T(8,128)}, f32[64,64]{0,1:T(8,128)S(1)}, u32[]{:S(2)}) copy-start(f32[64,64]{0,1:T(8,128)S(1)} %fusion.156) | copy-start | bytes 49156
  42.2 1.1 copy-start.15
  43.4 377.6 %all-to-all-start = ((bf16[64,1,6,1024]{3,2,1,0:T(8,128)(2,1)}), bf16[64,1,6,1024]{3,2,1,0:T(8,128)(2,1)S(1)}, u32[]{:S(2)}, u32[]{:S(2)}) async-start(bf16[64,1,6,1024]{3,2,1,0:T(8,128)(2,1)} %stack.3), calls=%async_computation | async-start | bytes 2097152 | tf_op jit(solution)/shard_map/all_to_all | solution.py:145
  421.0 1.7 copy-start
  422.8 1.0 copy-start.2
  424.0 0.7 copy-start.28
  424.7 0.7 copy-start.20
  426.1 1.0 copy-start.4
  427.3 0.7 copy-start.21
  429.2 2.4 copy-start.22
  439.1 1.2 copy-start.3
  439.1 1.4 copy-start.6
  440.4 20.8 %copy-start.8 = (bf16[256,1024]{1,0:T(8,128)(2,1)S(1)}, bf16[256,1024]{1,0:T(8,128)(2,1)}, u32[]{:S(2)}) copy-start(bf16[256,1024]{1,0:T(8,128)(2,1)} %param.17) | copy-start | bytes 1572868
  461.2 35.4 %copy-start.16 = (f32[1,64,512]{2,1,0:T(8,128)S(1)}, f32[1,64,512]{2,1,0:T(8,128)}, u32[]{:S(2)}) copy-start(f32[1,64,512]{2,1,0:T(8,128)} %convolution_bitcast_fusion) | copy-start | bytes 393220
  462.4 55.5 %all-to-all-start.1 = ((bf16[64,16,256]{2,1,0:T(8,128)(2,1)}), bf16[64,16,256]{2,1,0:T(8,128)(2,1)S(1)}, u32[]{:S(2)}, u32[]{:S(2)}) async-start(bf16[64,16,256]{2,1,0:T(8,128)(2,1)} %bitcast.27), calls=%async_computation.1 | async-start | bytes 1048576 | tf_op jit(solution)/shard_map/all_to_all | solution.py:171
  512.1 6.7 %copy-start.23 = (pred[64]{0:T(512)(128)(4,1)S(1)}, pred[64]{0:T(512)(128)(4,1)}, u32[]{:S(2)}) copy-start(pred[64]{0:T(512)(128)(4,1)} %compare_and_fusion.1) | copy-start | bytes 196
  517.9 1.4 copy-start.13
  519.1 1.3 copy-start.10
  544.8 7.8 %copy-start.5 = (f32[64,512]{1,0:T(8,128)S(1)}, f32[64,512]{1,0:T(8,128)}, u32[]{:S(2)}) copy-start(f32[64,512]{1,0:T(8,128)} %convolution_subtract_fusion.2) | copy-start | bytes 393220
  575.9 7.6 %copy-start.14 = (f32[64,64]{0,1:T(8,128)S(1)}, f32[64,64]{0,1:T(8,128)}, u32[]{:S(2)}) copy-start(f32[64,64]{0,1:T(8,128)} %copy-done.12) | copy-start | bytes 49156
  583.5 1.6 copy-start.11
  586.8 0.7 copy-start.25
  587.4 1.7 copy-start.24
  588.2 14.6 %copy-start.7 = (bf16[256,1024]{1,0:T(8,128)(2,1)S(1)}, bf16[256,1024]{1,0:T(8,128)(2,1)}, u32[]{:S(2)}) copy-start(bf16[256,1024]{1,0:T(8,128)(2,1)} %param.16) | copy-start | bytes 1572868
  590.1 30.8 %all-to-all-start.3 = ((bf16[16,64,256]{2,0,1:T(8,128)(2,1)}), bf16[16,64,256]{2,0,1:T(8,128)(2,1)S(1)}, u32[]{:S(2)}, u32[]{:S(2)}) async-start(bf16[16,64,256]{2,0,1:T(8,128)(2,1)} %select_bitcast_fusion), calls=%async_computation.3 | async-start | bytes 1048576 | tf_op jit(solution)/shard_map/all_to_all | solution.py:182
Sparse Core Ops, SparseCore 0:
  12.2 218.4 all-gather.5
